TPU v7x, 256 devices: a whole 4x4x8 slice. The times are simulated.
256 devices in a mesh: param: 32 (over y, x, core), walker: 8 (over z).
Axes of the slice: x: 4, y: 4, z: 8, core: 2. Of those that a mesh axis runs over, the one named last changes fastest.
Arguments:
- derivs: float32 [64, 4980736], P('walker', 'param'), may hold values from -1.7 to 1.7
- gradient: float32 [4980736], P('param'), may hold values from -0.01171875 to 0.01171875
Outputs:
- solution: float32 [4980736], P(('param', 'walker'))
All inputs are finite; a program needn't handle non-finite values.
Results may differ from a plain program's by a relative error of at most 0.0003.
Values sent between devices are 32-bit elements; how exact they have to be, the bound alone decides.
A program may use at most 64 MiB of HBM per device.

v0:
```python
import jax
import jax.numpy as jnp
from jax import lax
from jax.sharding import PartitionSpec as P

ITERS = 3


DAMPING = 0.001


def body(derivs, gradient):
    walkers = lax.axis_size("walker")
    rows_all = derivs.shape[0] * walkers
    share_len = gradient.shape[0] // walkers
    offset = lax.axis_index("walker") * share_len

    def own_share(vector):
        return lax.dynamic_slice_in_dim(vector, offset, share_len, 0)

    def local_view(vector):
        return own_share(vector)

    def squares(vector):
        return lax.psum(jnp.sum(vector * vector), ("param", "walker"))

    solution = jnp.zeros_like(gradient)
    residual = gradient
    direction = gradient
    norm_now = squares(local_view(gradient))
    for step_idx in range(ITERS):
        row_part = jnp.dot(derivs, direction, precision=lax.Precision.HIGHEST)
        row_vals = lax.psum(row_part, "param")
        back_vals = lax.psum(jnp.dot(row_vals, derivs, precision=lax.Precision.HIGHEST), "walker")
        image = back_vals / rows_all + DAMPING * direction
        advance_solution = solution
        advance_residual = residual
        dir_view = local_view(direction)
        img_view = local_view(image)
        curv_pq = lax.psum(jnp.sum(dir_view * img_view), ("param", "walker"))
        step_len = norm_now / curv_pq
        advance_residual = advance_residual - step_len * image
        norm_next = squares(local_view(advance_residual))
        advance_solution = advance_solution + step_len * direction
        solution, residual, norm_next = (advance_solution, advance_residual, norm_next)
        direction = residual + norm_next / norm_now * direction
        norm_now = norm_next
    return own_share(solution)


def solution(mesh):
    in_specs = (P("walker", "param"), P("param"))
    out_specs = P(("param", "walker"))
    return jax.shard_map(body, mesh=mesh, in_specs=in_specs, out_specs=out_specs, check_vma=False)
```

profile of v0, /device:TPU:1, one launch (start us, length us, event | category | flops | bytes accessed | tf_op | source)
XLA Modules:
  0.0 868.1 jit_solution(3013263644539260570)
XLA Ops:
  6.5 0.0 all-reduce.5.cloned.1.call-start
  6.5 0.0 copy-start
  6.5 13.8 %convolution_bitcast_fusion.2 = f32[8]{0:T(128)S(1)} fusion(f32[8,155648]{1,0:T(8,128)} %param.2, f32[155648,1]{0,1:T(1,128)} %bitcast.30), kind=kOutput, calls=%fused_computation.2 | convolution fusion | flops 14942208 | bytes 5603360 | tf_op jit(solution)/shard_map/dot_general | solution.py:32
  20.3 65.4 %psum.85 = f32[8]{0:T(128)S(1)} all-reduce(f32[8]{0:T(128)S(1)} %convolution_bitcast_fusion.2), channel_id=1, replica_groups=mesh['param'=32,'walker'=8] {'param'}, use_global_device_ids=true, to_apply=%region_2.0 | all-reduce | flops 8 | bytes 64 | tf_op jit(solution)/shard_map/psum | solution.py:33
  85.7 7.7 fusion.7
  93.4 0.0 all-reduce.5.cloned.1.call-update
  93.5 0.0 all-reduce.7.cloned.1.call-start
  93.5 70.1 %all-reduce.5.cloned.1.call-done = f32[155648]{0:T(1024)} async-done(((f32[155648]{0:T(1024)}), f32[155648]{0:T(1024)}) %all-reduce.5.cloned.1.call-update) | async-done | bytes 622608 | tf_op jit(solution)/shard_map/psum | solution.py:34
  163.6 0.0 copy-done
  163.6 1.2 multiply_add_fusion.3
  164.8 0.6 multiply_reduce_fusion.3
  165.4 79.8 %all-reduce = (f32[]{:T(128)}, f32[]{:T(128)}) all-reduce(f32[]{:T(128)} %get-tuple-element.6, f32[]{:T(128)} %get-tuple-element.5), channel_id=1, replica_groups=mesh['param'=32,'walker'=8] {'param','walker'}, use_global_device_ids=true, to_apply=%region_1.0 | all-reduce | flops 2 | bytes 16 | tf_op jit(solution)/shard_map/psum | solution.py:25
  246.6 1.2 multiply_subtract_fusion.1
  247.8 0.6 multiply_reduce_fusion.2
  248.4 73.4 %psum.88 = f32[]{:T(128)} all-reduce(f32[]{:T(128)} %multiply_reduce_fusion.2), channel_id=1, replica_groups=mesh['param'=32,'walker'=8] {'param','walker'}, use_global_device_ids=true, to_apply=%region_7.0 | all-reduce | flops 1 | bytes 8 | tf_op jit(solution)/shard_map/psum | solution.py:25
  323.1 0.1 multiply_add_fusion.2
  323.2 12.7 %convolution_bitcast_fusion.1 = f32[8]{0:T(128)S(1)} fusion(f32[155648,1]{0,1:T(1,128)S(1)} %bitcast.31, f32[8,155648]{1,0:T(8,128)} %param.2), kind=kOutput, calls=%fused_computation.1 | convolution fusion | flops 14942208 | bytes 5603360 | tf_op jit(solution)/shard_map/dot_general | solution.py:32
  335.9 62.9 %psum.89 = f32[8]{0:T(128)S(1)} all-reduce(f32[8]{0:T(128)S(1)} %convolution_bitcast_fusion.1), channel_id=1, replica_groups=mesh['param'=32,'walker'=8] {'param'}, use_global_device_ids=true, to_apply=%region_8.0 | all-reduce | flops 8 | bytes 64 | tf_op jit(solution)/shard_map/psum | solution.py:33
  398.8 7.7 fusion.5
  406.5 0.0 all-reduce.7.cloned.1.call-update
  406.5 0.0 all-reduce.9.cloned.1.call-start
  406.5 65.1 %all-reduce.7.cloned.1.call-done = f32[155648]{0:T(1024)} async-done(((f32[155648]{0:T(1024)}), f32[155648]{0:T(1024)}) %all-reduce.7.cloned.1.call-update) | async-done | bytes 622608 | tf_op jit(solution)/shard_map/psum | solution.py:34
  471.6 1.2 multiply_add_fusion.1
  472.8 0.7 multiply_reduce_fusion.1
  473.5 79.7 %psum.91 = f32[]{:T(128)} all-reduce(f32[]{:T(128)} %multiply_reduce_fusion.1), channel_id=1, replica_groups=mesh['param'=32,'walker'=8] {'param','walker'}, use_global_device_ids=true, to_apply=%region_11.0 | all-reduce | flops 1 | bytes 8 | tf_op jit(solution)/shard_map/psum | solution.py:40
  554.6 0.1 multiply_subtract_fusion
  554.7 0.6 multiply_reduce_fusion
  555.3 73.4 %psum.92 = f32[]{:T(128)} all-reduce(f32[]{:T(128)} %multiply_reduce_fusion), channel_id=1, replica_groups=mesh['param'=32,'walker'=8] {'param','walker'}, use_global_device_ids=true, to_apply=%region_13.0 | all-reduce | flops 1 | bytes 8 | tf_op jit(solution)/shard_map/psum | solution.py:25
  630.0 0.1 multiply_add_fusion
  630.1 12.7 %convolution_bitcast_fusion = f32[8]{0:T(128)S(1)} fusion(f32[155648,1]{0,1:T(1,128)S(1)} %bitcast.32, f32[8,155648]{1,0:T(8,128)} %param.2), kind=kOutput, calls=%fused_computation | convolution fusion | flops 14942208 | bytes 5603360 | tf_op jit(solution)/shard_map/dot_general | solution.py:32
  642.7 62.9 %psum.93 = f32[8]{0:T(128)S(1)} all-reduce(f32[8]{0:T(128)S(1)} %convolution_bitcast_fusion), channel_id=1, replica_groups=mesh['param'=32,'walker'=8] {'param'}, use_global_device_ids=true, to_apply=%region_14.0 | all-reduce | flops 8 | bytes 64 | tf_op jit(solution)/shard_map/psum | solution.py:33
  705.6 7.7 fusion.3
  713.3 0.0 all-reduce.9.cloned.1.call-update
  713.4 65.1 %all-reduce.9.cloned.1.call-done = f32[155648]{0:T(1024)} async-done(((f32[155648]{0:T(1024)}), f32[155648]{0:T(1024)}) %all-reduce.9.cloned.1.call-update) | async-done | bytes 622608 | tf_op jit(solution)/shard_map/psum | solution.py:34
  778.4 1.5 fusion.2
  780.0 79.7 %psum.95 = f32[]{:T(128)} all-reduce(f32[]{:T(128)} %fusion.2), channel_id=1, replica_groups=mesh['param'=32,'walker'=8] {'param','walker'}, use_global_device_ids=true, to_apply=%region_17.0 | all-reduce | flops 1 | bytes 8 | tf_op jit(solution)/shard_map/psum | solution.py:40
  860.9 0.7 multiply_add_fusion.4
Async XLA Ops:
  6.5 157.1 %all-reduce.5.cloned.1.call-start = ((), (), s32[]{:S(2)}) async-start(), calls=%async_computation | async-start | bytes 1245184 | tf_op jit(solution)/shard_map/psum | solution.py:34
  6.5 157.1 %copy-start = (f32[155648]{0:T(1024)S(1)}, f32[155648]{0:T(1024)}, u32[]{:S(2)}) copy-start(f32[155648]{0:T(1024)} %param.3) | copy-start | bytes 1867780
  93.5 378.2 %all-reduce.7.cloned.1.call-start = ((), (), s32[]{:S(2)}) async-start(), calls=%async_computation.1 | async-start | bytes 1245184 | tf_op jit(solution)/shard_map/psum | solution.py:34
  406.5 372.0 %all-reduce.9.cloned.1.call-start = ((), (), s32[]{:S(2)}) async-start(), calls=%async_computation.2 | async-start | bytes 1245184 | tf_op jit(solution)/shard_map/psum | solution.py:34
Sparse Core Ops, SparseCore 0:
  93.6 70.0 all-reduce.4
  406.6 64.9 all-reduce.6
  713.5 64.9 all-reduce.8
where the time goes:
time: 869 us; the launch traced here: 868 us
  blocking collectives  577 us (66%)
  waiting for transfers between devices  200 us (23%)
  matrix products  62.1 us (7%)
  between operations  19.8 us (2%)
    psum x3, blocking collectives, squares(): return lax.psum(jnp.sum(vector * vector), ('param', 'walker'))  227 us
    psum x3, waiting for transfers between devices, body(): lax.psum(jnp.dot(row_vals, derivs, precision=lax.Precision.HIGHEST), 'wal...  200 us
    psum x3, blocking collectives, body(): row_vals = lax.psum(row_part, 'param')  191 us
    psum x2, blocking collectives, body(): curv_pq = lax.psum(jnp.sum(dir_view * img_view), ('param', 'walker'))  159 us
    dot_general x3, matrix products, body(): row_part = jnp.dot(derivs, direction, precision=lax.Precision.HIGHEST)  39.1 us
    dot_general x3, matrix products, body(): jnp.dot(row_vals, derivs, precision=lax.Precision.HIGHEST)  23.1 us
  transfers between devices with their start and end apart: 3, of which 3 were waited for; matrix products, arithmetic and copies ran while one was open for 0% of the time, Pallas kernels for 0%

commit v1 on v0

v1 whole, which is shorter than its diff:
```python
import functools

import jax
import jax.numpy as jnp
from jax import lax
from jax.experimental import pallas as pl
from jax.experimental.pallas import tpu as pltpu
from jax.sharding import PartitionSpec as P

DAMPING = 0.001
LANES = 128
MESH = pl.DeviceIdType.MESH


def kernel(cfg, d_hbm, g_hbm, x_ref, dv, gv, t1, t2, r1f, r2f, rb, acc,
           msg, gath, wbuf, zmsg, zgath,
           load_sem, ring_send, ring_recv, pl_send, pl_recv, z_send, z_recv):
    n_p, n_z, rows, sh, cut, rows_all = cfg
    me_p = lax.axis_index("param")
    me_z = lax.axis_index("walker")
    groups = sh // 8
    right = lax.rem(me_z + 1, n_z)
    left = lax.rem(me_z + n_z - 1, n_z)

    def base(k):
        return pl.multiple_of(lax.rem(me_z + (k + n_z), n_z) * sh, 8)

    barrier = pltpu.get_barrier_semaphore()

    def greet_p(i, c):
        pl.semaphore_signal(barrier, inc=1, device_id={"param": lax.rem(me_p + i, n_p)}, device_id_type=MESH)
        return c

    def greet_z(i, c):
        pl.semaphore_signal(barrier, inc=1, device_id={"walker": lax.rem(me_z + i, n_z)}, device_id_type=MESH)
        return c

    gcopy = pltpu.make_async_copy(g_hbm, gv, load_sem.at[n_z, 0])
    gcopy.start()
    loads = []
    for k in range(n_z):
        for r in range(rows):
            c = pltpu.make_async_copy(d_hbm.at[pl.ds(k * sh, sh), r, :], dv.at[r, pl.ds(k * sh, sh), :], load_sem.at[k, r])
            c.start()
            loads.append(c)
    lax.fori_loop(1, n_p, greet_p, 0)
    lax.fori_loop(1, n_z, greet_z, 0)

    def accum(b, vec, others, first):
        n = rows + 1 + len(others)
        if first:
            a = [jnp.zeros((8, LANES), jnp.float32) for _ in range(n)]
        else:
            a = [acc[i] for i in range(n)]

        def step(i, a):
            o = pl.multiple_of(b + i * 8, 8)
            v = vec[pl.ds(o, 8), :]
            out = [a[r] + dv[r, pl.ds(o, 8), :] * v for r in range(rows)]
            out.append(a[rows] + v * v)
            for j, ref in enumerate(others):
                out.append(a[rows + 1 + j] + ref[pl.ds(o, 8), :] * v)
            return tuple(out)

        a = lax.fori_loop(0, groups, step, tuple(a), unroll=True)
        for i in range(n):
            acc[i] = a[i]

    sub = lax.broadcasted_iota(jnp.int32, (16, LANES), 0)
    lane = lax.broadcasted_iota(jnp.int32, (16, LANES), 1)
    diag = sub == lane

    def plane_sum(it):
        part = jnp.sum(acc[...], axis=1)
        part = jnp.sum(part, axis=1, keepdims=True)
        row = jnp.sum(jnp.where(diag, part, 0.0), axis=0, keepdims=True)
        msg[it] = row
        gath[it, me_p] = row

        def send(i, c):
            peer = lax.rem(me_p + i, n_p)
            pltpu.make_async_remote_copy(msg.at[it], gath.at[it, me_p], pl_send.at[it], pl_recv.at[it],
                                         device_id={"param": peer}, device_id_type=MESH).start()
            return c

        lax.fori_loop(1, n_p, send, 0)
        every = gath.at[it, pl.ds(0, n_p - 1)]
        pltpu.make_async_copy(every, every, pl_recv.at[it]).wait()
        tot = jnp.sum(gath[it, :, 0, :], axis=0, keepdims=True)
        tot = jnp.sum(jnp.where(diag, tot, 0.0), axis=1, keepdims=True)
        return jnp.broadcast_to(tot, (16, LANES))

    def z_start(it, w):
        row = jnp.sum(w * w, axis=0, keepdims=True)
        zmsg[it] = row
        zgath[it, me_z] = row

        def send(i, c):
            peer = lax.rem(me_z + i, n_z)
            pltpu.make_async_remote_copy(zmsg.at[it], zgath.at[it, me_z], z_send.at[it], z_recv.at[it],
                                         device_id={"walker": peer}, device_id_type=MESH).start()
            return c

        lax.fori_loop(1, n_z, send, 0)

    def z_finish(it):
        every = zgath.at[it, pl.ds(0, n_z - 1)]
        pltpu.make_async_copy(every, every, z_recv.at[it]).wait()
        return jnp.sum(zgath[it, :, 0, :], axis=0, keepdims=True)

    def project(k, t, w):
        b = base(k)

        def step(i, c):
            o = pl.multiple_of(b + i * 8, 8)
            s = dv[0, pl.ds(o, 8), :] * w[0]
            for r in range(1, rows):
                s = s + dv[r, pl.ds(o, 8), :] * w[r]
            t[pl.ds(o, 8), :] = s
            return c

        lax.fori_loop(0, groups, step, 0, unroll=True)

    half = ((0, cut), (cut, sh - cut))

    def ring(it, phase, way, s, c, src, dst):
        return pltpu.make_async_remote_copy(
            src, dst, ring_send.at[it, phase, way, s, c], ring_recv.at[it, phase, way, s, c],
            device_id={"walker": right if way == 0 else left}, device_id_type=MESH)

    steps = n_z // 2

    def reduce_scatter(it, t, w):
        wv = [jnp.broadcast_to(w[r:r + 1, :], (8, LANES)) for r in range(rows)]
        sends = {}

        def send(way, s, c):
            sign = 1 if way == 0 else -1
            lo, n = half[c]
            b = base(sign * (steps - s))
            cp = ring(it, 0, way, s, c, t.at[pl.ds(b + lo, n), :], rb.at[it, way, s, pl.ds(lo, n), :])
            cp.start()
            sends[way, s, c] = cp

        def add(way, s, c):
            sends[way, s, c].wait_recv()
            sign = 1 if way == 0 else -1
            lo, n = half[c]
            b = pl.multiple_of(base(sign * (steps - s - 1)) + lo, 8)
            t[pl.ds(b, n), :] += rb[it, way, s, pl.ds(lo, n), :]

        project(steps, t, wv)
        send(0, 0, 0)
        send(1, 0, 1)
        project(steps - 1, t, wv)
        send(0, 1, 1)
        project(1 - steps, t, wv)
        send(1, 1, 0)
        for k in range(steps - 2, 0, -1):
            project(k, t, wv)
            project(-k, t, wv)
        project(0, t, wv)
        for s in range(1, steps):
            for way in range(2):
                add(way, s - 1, way)
                send(way, s, way)
            for way in range(2):
                add(way, s, 1 - way)
                if s + 1 < steps:
                    send(way, s + 1, 1 - way)
        for way in range(2):
            add(way, steps - 1, way)
        for cp in sends.values():
            cp.wait_send()

    def all_gather(it, rf, others):
        sends = {}

        def send(way, s, c):
            sign = 1 if way == 0 else -1
            lo, n = half[c]
            piece = rf.at[pl.ds(base(-sign * s) + lo, n), :]
            cp = ring(it, 1, way, s, c, piece, piece)
            cp.start()
            sends[way, s, c] = cp

        for way in range(2):
            send(way, 0, way)
        for way in range(2):
            send(way, 0, 1 - way)
        accum(base(0), rf, others, True)
        for s in range(steps):
            for way in range(2):
                sends[way, s, way].wait_recv()
                if s + 1 < steps:
                    send(way, s + 1, way)
            if s + 1 < steps:
                for way in range(2):
                    sends[way, s, 1 - way].wait_recv()
                    if s + 2 < steps:
                        send(way, s + 1, 1 - way)
                accum(base(-1 - s), rf, others, False)
                accum(base(1 + s), rf, others, False)
            else:
                accum(base(steps), rf, others, False)
        for cp in sends.values():
            cp.wait_send()

    own = pl.ds(base(0), sh)
    inv = 1.0 / rows_all

    acc[...] = jnp.zeros_like(acc)
    gcopy.wait()
    for k in range(n_z):
        for r in range(rows):
            loads[k * rows + r].wait()
        accum(k * sh, gv, (), k == 0)
    pl.semaphore_wait(barrier, n_p - 1 + n_z - 1)

    tot = plane_sum(0)
    w0, rr0 = tot[:rows], tot[rows:rows + 1]
    pp0 = rr0
    z_start(0, w0)
    reduce_scatter(0, t1, w0)
    a0 = rr0 / (z_finish(0) * inv + DAMPING * pp0)
    r1f[own, :] = gv[own, :] - a0 * (t1[own, :] * inv + DAMPING * gv[own, :])

    all_gather(0, r1f, (gv,))
    tot = plane_sum(1)
    rr1, rp1 = tot[rows:rows + 1], tot[rows + 1:rows + 2]
    b0 = rr1 / rr0
    u1 = tot[:rows]
    w1 = u1 + b0 * w0
    pp1 = rr1 + b0 * (2.0 * rp1 + b0 * pp0)
    z_start(1, w1)
    reduce_scatter(1, t2, u1)
    a1 = rr1 / (z_finish(1) * inv + DAMPING * pp1)
    p1 = r1f[own, :] + b0 * gv[own, :]
    r2f[own, :] = r1f[own, :] - a1 * ((t2[own, :] + b0 * t1[own, :]) * inv + DAMPING * p1)

    all_gather(1, r2f, (gv, r1f))
    tot = plane_sum(2)
    rr2, rg2, rq2 = tot[rows:rows + 1], tot[rows + 1:rows + 2], tot[rows + 2:rows + 3]
    b1 = rr2 / rr1
    w2 = tot[:rows] + b1 * w1
    pp2 = rr2 + b1 * (2.0 * (rq2 + b0 * rg2) + b1 * pp1)
    z_start(2, w2)
    a2 = rr2 / (z_finish(2) * inv + DAMPING * pp2)
    p1 = r1f[own, :] + b0 * gv[own, :]
    p2 = r2f[own, :] + b1 * p1
    x_ref[...] = a0 * gv[own, :] + a1 * p1 + a2 * p2

    for it in range(3):
        every = gath.at[it, pl.ds(0, n_p - 1)]
        pltpu.make_async_copy(every, every, pl_send.at[it]).wait()
        every = zgath.at[it, pl.ds(0, n_z - 1)]
        pltpu.make_async_copy(every, every, z_send.at[it]).wait()


def body(derivs, gradient):
    n_p, n_z = lax.axis_size("param"), lax.axis_size("walker")
    rows, cols = derivs.shape
    tiles = cols // LANES
    sh = tiles // n_z
    cut = (sh // 2 + 7) // 8 * 8
    d = derivs.reshape(rows, tiles, LANES).transpose(1, 0, 2)
    g = gradient.reshape(tiles, LANES)
    f32 = jnp.float32
    full = pltpu.VMEM((tiles, LANES), f32)
    steps = n_z // 2
    x = pl.pallas_call(
        functools.partial(kernel, (n_p, n_z, rows, sh, cut, rows * n_z)),
        out_shape=jax.ShapeDtypeStruct((sh, LANES), f32),
        in_specs=[pl.BlockSpec(memory_space=pltpu.HBM)] * 2,
        out_specs=pl.BlockSpec(memory_space=pltpu.VMEM),
        scratch_shapes=[
            pltpu.VMEM((rows, tiles, LANES), f32),
            full, full, full, full, full,
            pltpu.VMEM((2, 2, steps, sh, LANES), f32),
            pltpu.VMEM((16, 8, LANES), f32),
            pltpu.VMEM((3, 1, LANES), f32),
            pltpu.VMEM((3, n_p, 1, LANES), f32),
            pltpu.VMEM((16, LANES), f32),
            pltpu.VMEM((3, 1, LANES), f32),
            pltpu.VMEM((3, n_z, 1, LANES), f32),
            pltpu.SemaphoreType.DMA((n_z + 1, rows)),
            pltpu.SemaphoreType.DMA((2, 2, 2, steps, 2)),
            pltpu.SemaphoreType.DMA((2, 2, 2, steps, 2)),
            pltpu.SemaphoreType.DMA((3,)),
            pltpu.SemaphoreType.DMA((3,)),
            pltpu.SemaphoreType.DMA((3,)),
            pltpu.SemaphoreType.DMA((3,)),
        ],
        compiler_params=pltpu.CompilerParams(
            collective_id=0, has_side_effects=True, vmem_limit_bytes=40 * 1024 * 1024),
        name="cg_solve",
    )(d, g)
    return x.reshape(sh * LANES)


def solution(mesh):
    in_specs = (P("walker", "param"), P("param"))
    out_specs = P(("param", "walker"))
    return jax.shard_map(body, mesh=mesh, in_specs=in_specs, out_specs=out_specs, check_vma=False)
```

time: 869 us -> 93.5 us (0.11)
  blocking collectives: 577 us -> 0 us
  waiting for transfers between devices: 200 us -> 0 us
  Pallas kernels: 0 us -> 89.2 us
  matrix products: 62.1 us -> 0 us
  between operations: 19.8 us -> 0.01 us
    psum x8 -> x0, blocking collectives: 577 us -> none  [the longest x3 227 us: squares(): return lax.psum(jnp.sum(vector * vector), ('param', 'walker'))]
    psum x3 -> x0, waiting for transfers between devices: 200 us -> none  [body(): lax.psum(jnp.dot(row_vals, derivs, precision=lax.Precision.HIGHEST), 'wal...]
    pallas_call x0 -> x1, Pallas kernels: none -> 89.2 us  [body(): pl.pallas_call(functools.partial(kernel, (n_p, n_z, rows, sh, cut, rows *...]
    dot_general x6 -> x0, matrix products: 62.1 us -> none  [the longest x3 39.1 us: body(): row_part = jnp.dot(derivs, direction, precision=lax.Precision.HIGHEST)]
  transfers between devices with their start and end apart: 3 -> 0, of which waited for: 3 -> 0; matrix products, arithmetic and copies ran while one was open for 0% -> 0% of each run, Pallas kernels for 0% -> 0%
where the time goes in v1:
time: 93.5 us; the launch traced here: 93.3 us
  Pallas kernels  89.2 us (95%)
  local copies, waits for them, and re-layouts  4.13 us (4%)
    pallas_call x1, Pallas kernels, body(): pl.pallas_call(functools.partial(kernel, (n_p, n_z, rows, sh, cut, rows *...  89.2 us
    unnamed x5, local copies, waits for them, and re-layouts  4.13 us

profile of v1, /device:TPU:1, one launch (start us, length us, event | category | flops | bytes accessed | tf_op | source)
XLA Modules:
  0.0 93.3 jit_solution(3536121686720235523)
XLA Ops:
  0.0 0.0 copy-start
  0.0 2.4 %copy-done = f32[8,155648]{1,0:T(8,128)S(1)} copy-done((f32[8,155648]{1,0:T(8,128)S(1)}, f32[8,155648]{1,0:T(8,128)}, u32[]{:S(2)}) %copy-start) | copy-done | bytes 4980760
  2.4 0.0 copy-start.1
  2.4 1.1 %copy-done.1 = f32[155648]{0:T(1024)S(1)} copy-done((f32[155648]{0:T(1024)S(1)}, f32[155648]{0:T(1024)}, u32[]{:S(2)}) %copy-start.1) | copy-done | bytes 622616
  3.5 89.2 %cg_solve.1 = f32[152,128]{1,0:T(8,128)S(1)} custom-call(f32[1216,8,128]{2,1,0:T(8,128)S(1)} %bitcast.5, f32[1216,128]{1,0:T(8,128)S(1)} %bitcast.6), custom_call_target="tpu_custom_call" | custom-call | tf_op jit(solution)/shard_map/cg_solve/pallas_call | solution.py:271
  92.7 0.6 copy.4
Async XLA Ops:
  0.0 2.4 %copy-start = (f32[8,155648]{1,0:T(8,128)S(1)}, f32[8,155648]{1,0:T(8,128)}, u32[]{:S(2)}) copy-start(f32[8,155648]{1,0:T(8,128)} %param.2) | copy-start | bytes 14942212
  2.4 1.1 %copy-start.1 = (f32[155648]{0:T(1024)S(1)}, f32[155648]{0:T(1024)}, u32[]{:S(2)}) copy-start(f32[155648]{0:T(1024)} %param.3) | copy-start | bytes 1867780

commit v2 on v1

v2 whole, which is shorter than its diff:
```python
import functools

import jax
import jax.numpy as jnp
from jax import lax
from jax.experimental import pallas as pl
from jax.experimental.pallas import tpu as pltpu
from jax.sharding import PartitionSpec as P

DAMPING = 0.001
PIECES = 4
LANES = 128
MESH = pl.DeviceIdType.MESH


def kernel(cfg, d_hbm, g_hbm, x_ref, dv, gv, t1, t2, r1f, r2f, rb, acc,
           msg, gath, zmsg, zgath,
           load_sem, ring_send, ring_recv, pl_send, pl_recv, z_send, z_recv):
    n_p, n_z, rows, sh, cuts, rows_all = cfg
    me_p = lax.axis_index("param")
    me_z = lax.axis_index("walker")
    groups = sh // 8

    def base(k):
        return pl.multiple_of(lax.rem(me_z + (k + n_z), n_z) * sh, 8)

    barrier = pltpu.get_barrier_semaphore()

    def greet_p(i, c):
        pl.semaphore_signal(barrier, inc=1, device_id={"param": lax.rem(me_p + i, n_p)}, device_id_type=MESH)
        return c

    def greet_z(i, c):
        pl.semaphore_signal(barrier, inc=1, device_id={"walker": lax.rem(me_z + i, n_z)}, device_id_type=MESH)
        return c

    lax.fori_loop(1, n_p, greet_p, 0)
    lax.fori_loop(1, n_z, greet_z, 0)

    gcopy = pltpu.make_async_copy(g_hbm, gv, load_sem.at[n_z, 0])
    gcopy.start()
    loads = []
    for k in range(n_z):
        for r in range(rows):
            c = pltpu.make_async_copy(d_hbm.at[pl.ds(k * sh, sh), r, :], dv.at[r, pl.ds(k * sh, sh), :], load_sem.at[k, r])
            c.start()
            loads.append(c)

    def accum(vec, others):
        n = rows + 1 + len(others)

        def shard(k, a):
            out = list(a)
            for i in range(groups):
                o = pl.multiple_of(k * sh + i * 8, 8)
                v = vec[pl.ds(o, 8), :]
                for r in range(rows):
                    out[r] = out[r] + dv[r, pl.ds(o, 8), :] * v
                out[rows] = out[rows] + v * v
                for j, ref in enumerate(others):
                    out[rows + 1 + j] = out[rows + 1 + j] + ref[pl.ds(o, 8), :] * v
            return tuple(out)

        a = lax.fori_loop(0, n_z, shard, tuple(jnp.zeros((8, LANES), jnp.float32) for _ in range(n)))
        for i in range(n):
            acc[i] = a[i]

    sub = lax.broadcasted_iota(jnp.int32, (16, LANES), 0)
    lane = lax.broadcasted_iota(jnp.int32, (16, LANES), 1)
    diag = sub == lane

    def plane_sum(it):
        part = jnp.sum(acc[...], axis=1)
        part = jnp.sum(part, axis=1, keepdims=True)
        row = jnp.sum(jnp.where(diag, part, 0.0), axis=0, keepdims=True)
        msg[it] = row
        gath[it, me_p] = row

        def send(i, c):
            peer = lax.rem(me_p + i, n_p)
            pltpu.make_async_remote_copy(msg.at[it], gath.at[it, me_p], pl_send.at[it], pl_recv.at[it],
                                         device_id={"param": peer}, device_id_type=MESH).start()
            return c

        lax.fori_loop(1, n_p, send, 0)
        every = gath.at[it, pl.ds(0, n_p - 1)]
        pltpu.make_async_copy(every, every, pl_recv.at[it]).wait()
        tot = jnp.sum(gath[it, :, 0, :], axis=0, keepdims=True)
        tot = jnp.sum(jnp.where(diag, tot, 0.0), axis=1, keepdims=True)
        return jnp.broadcast_to(tot, (16, LANES))

    def z_start(it, w):
        row = jnp.sum(w * w, axis=0, keepdims=True)
        zmsg[it] = row
        zgath[it, me_z] = row

        def send(i, c):
            peer = lax.rem(me_z + i, n_z)
            pltpu.make_async_remote_copy(zmsg.at[it], zgath.at[it, me_z], z_send.at[it], z_recv.at[it],
                                         device_id={"walker": peer}, device_id_type=MESH).start()
            return c

        lax.fori_loop(1, n_z, send, 0)

    def z_finish(it):
        every = zgath.at[it, pl.ds(0, n_z - 1)]
        pltpu.make_async_copy(every, every, z_recv.at[it]).wait()
        return jnp.sum(zgath[it, :, 0, :], axis=0, keepdims=True)

    def project(first, count, t, wv):
        def shard(k, c):
            b = base(first + k)
            for i in range(groups):
                o = pl.multiple_of(b + i * 8, 8)
                s = dv[0, pl.ds(o, 8), :] * wv[0]
                for r in range(1, rows):
                    s = s + dv[r, pl.ds(o, 8), :] * wv[r]
                t[pl.ds(o, 8), :] = s
            return c

        lax.fori_loop(0, count, shard, 0)

    pieces = tuple((cuts[c], cuts[c + 1] - cuts[c]) for c in range(len(cuts) - 1))
    n_c = len(pieces)
    far = (range(n_c // 2), range(n_c // 2, n_c))
    signs = (1, -1)

    def ring(it, phase, way, kind, c, hops, src, dst):
        return pltpu.make_async_remote_copy(
            src, dst, ring_send.at[it, phase], ring_recv.at[it, phase, way, kind, c],
            device_id={"walker": lax.rem(me_z + n_z + signs[way] * hops, n_z)}, device_id_type=MESH)

    def span(k, c):
        lo, n = pieces[c]
        return pl.ds(pl.multiple_of(base(k) + lo, 8), n)

    def reduce_scatter(it, t, w, finish):
        wv = [jnp.broadcast_to(w[r:r + 1, :], (8, LANES)) for r in range(rows)]

        def copy(way, kind, c, k, hops):
            lo, n = pieces[c]
            return ring(it, 0, way, kind, c, hops, t.at[span(signs[way] * k, c), :],
                        rb.at[it, way, kind, pl.ds(lo, n), :])

        def landed(way, kind, c):
            lo, n = pieces[c]
            return rb[it, way, kind, pl.ds(lo, n), :]

        project(3, 3, t, wv)
        for c in range(n_c):
            for way in range(2):
                if c in far[way]:
                    copy(way, 0, c, 4, 2).start()
            for way in range(2):
                copy(way, 1, c, 3, 1).start()
        project(6, 5, t, wv)
        for c in range(n_c):
            for way in range(2):
                copy(way, 2, c, 1, 1).start()
        for c in range(n_c):
            for way in range(2):
                copy(way, 1, c, 3, 1).wait_recv()
                s = landed(way, 1, c)
                if c in far[way]:
                    copy(way, 0, c, 4, 2).wait_recv()
                    s = s + landed(way, 0, c)
                t[span(signs[way] * 2, c), :] += s
                copy(way, 3, c, 2, 2).start()
        for c in range(n_c):
            s = t[span(0, c), :]
            for way in range(2):
                copy(way, 2, c, 1, 1).wait_recv()
                copy(way, 3, c, 2, 2).wait_recv()
                s = s + (landed(way, 2, c) + landed(way, 3, c))
            t[span(0, c), :] = s
            finish(c)

    def gather_copy(it, rf, way, kind, c, k, hops):
        piece = rf.at[span(-signs[way] * k, c), :]
        return ring(it, 1, way, kind, c, hops, piece, piece)

    def gather_start(it, rf, c):
        for way in range(2):
            gather_copy(it, rf, way, 0, c, 0, 2).start()
        for way in range(2):
            gather_copy(it, rf, way, 1, c, 0, 1).start()

    def gather_finish(it, rf):
        for c in range(n_c):
            for way in range(2):
                gather_copy(it, rf, way, 0, c, 0, 2).wait_recv()
                if c in far[way]:
                    gather_copy(it, rf, way, 3, c, 2, 2).start()
                gather_copy(it, rf, way, 2, c, 2, 1).start()
        for c in range(n_c):
            for way in range(2):
                gather_copy(it, rf, way, 1, c, 0, 1).wait_recv()
                gather_copy(it, rf, way, 2, c, 2, 1).wait_recv()
                if c in far[way]:
                    gather_copy(it, rf, way, 3, c, 2, 2).wait_recv()

    own = pl.ds(base(0), sh)
    inv = 1.0 / rows_all

    acc[...] = jnp.zeros_like(acc)
    gcopy.wait()
    for c in loads:
        c.wait()
    accum(gv, ())
    pl.semaphore_wait(barrier, n_p - 1 + n_z - 1)

    tot = plane_sum(0)
    w0, rr0 = tot[:rows], tot[rows:rows + 1]
    pp0 = rr0
    z_start(0, w0)
    a0 = []

    def residual1(c):
        if c == 0:
            a0.append(rr0 / (z_finish(0) * inv + DAMPING * pp0))
        at = span(0, c)
        r1f[at, :] = gv[at, :] - a0[0] * (t1[at, :] * inv + DAMPING * gv[at, :])
        gather_start(0, r1f, c)

    reduce_scatter(0, t1, w0, residual1)
    gather_finish(0, r1f)
    accum(r1f, (gv,))

    tot = plane_sum(1)
    rr1, rp1 = tot[rows:rows + 1], tot[rows + 1:rows + 2]
    b0 = rr1 / rr0
    u1 = tot[:rows]
    w1 = u1 + b0 * w0
    pp1 = rr1 + b0 * (2.0 * rp1 + b0 * pp0)
    z_start(1, w1)
    a1 = []

    def residual2(c):
        if c == 0:
            a1.append(rr1 / (z_finish(1) * inv + DAMPING * pp1))
        at = span(0, c)
        p1 = r1f[at, :] + b0 * gv[at, :]
        r2f[at, :] = r1f[at, :] - a1[0] * ((t2[at, :] + b0 * t1[at, :]) * inv + DAMPING * p1)
        gather_start(1, r2f, c)

    reduce_scatter(1, t2, u1, residual2)
    gather_finish(1, r2f)
    accum(r2f, (gv, r1f))

    tot = plane_sum(2)
    rr2, rg2, rq2 = tot[rows:rows + 1], tot[rows + 1:rows + 2], tot[rows + 2:rows + 3]
    b1 = rr2 / rr1
    w2 = tot[:rows] + b1 * w1
    pp2 = rr2 + b1 * (2.0 * (rq2 + b0 * rg2) + b1 * pp1)
    z_start(2, w2)
    p1 = r1f[own, :] + b0 * gv[own, :]
    x1 = a0[0] * gv[own, :] + a1[0] * p1
    p2 = r2f[own, :] + b1 * p1
    a2 = rr2 / (z_finish(2) * inv + DAMPING * pp2)
    x_ref[...] = x1 + a2 * p2

    sent = pl.ds(0, (n_z - 1) * sh)
    for it in range(2):
        for phase, ref in enumerate(((t1, t2)[it], (r1f, r2f)[it])):
            every = ref.at[sent, :]
            pltpu.make_async_copy(every, every, ring_send.at[it, phase]).wait()
    for it in range(3):
        every = gath.at[it, pl.ds(0, n_p - 1)]
        pltpu.make_async_copy(every, every, pl_send.at[it]).wait()
        every = zgath.at[it, pl.ds(0, n_z - 1)]
        pltpu.make_async_copy(every, every, z_send.at[it]).wait()


def body(derivs, gradient):
    n_p, n_z = lax.axis_size("param"), lax.axis_size("walker")
    rows, cols = derivs.shape
    tiles = cols // LANES
    sh = tiles // n_z
    cuts = tuple((sh // 8 * c + PIECES - 1) // PIECES * 8 for c in range(PIECES + 1))
    d = derivs.reshape(rows, tiles, LANES).transpose(1, 0, 2)
    g = gradient.reshape(tiles, LANES)
    f32 = jnp.float32
    full = pltpu.VMEM((tiles, LANES), f32)
    x = pl.pallas_call(
        functools.partial(kernel, (n_p, n_z, rows, sh, cuts, rows * n_z)),
        out_shape=jax.ShapeDtypeStruct((sh, LANES), f32),
        in_specs=[pl.BlockSpec(memory_space=pltpu.HBM)] * 2,
        out_specs=pl.BlockSpec(memory_space=pltpu.VMEM),
        scratch_shapes=[
            pltpu.VMEM((rows, tiles, LANES), f32),
            full, full, full, full, full,
            pltpu.VMEM((2, 2, 4, sh, LANES), f32),
            pltpu.VMEM((16, 8, LANES), f32),
            pltpu.VMEM((3, 1, LANES), f32),
            pltpu.VMEM((3, n_p, 1, LANES), f32),
            pltpu.VMEM((3, 1, LANES), f32),
            pltpu.VMEM((3, n_z, 1, LANES), f32),
            pltpu.SemaphoreType.DMA((n_z + 1, rows)),
            pltpu.SemaphoreType.DMA((2, 2)),
            pltpu.SemaphoreType.DMA((2, 2, 2, 4, PIECES)),
            pltpu.SemaphoreType.DMA((3,)),
            pltpu.SemaphoreType.DMA((3,)),
            pltpu.SemaphoreType.DMA((3,)),
            pltpu.SemaphoreType.DMA((3,)),
        ],
        compiler_params=pltpu.CompilerParams(
            collective_id=0, has_side_effects=True, vmem_limit_bytes=56 * 1024 * 1024),
        name="cg_solve",
    )(d, g)
    return x.reshape(sh * LANES)


def solution(mesh):
    in_specs = (P("walker", "param"), P("param"))
    out_specs = P(("param", "walker"))
    return jax.shard_map(body, mesh=mesh, in_specs=in_specs, out_specs=out_specs, check_vma=False)
```

time: 93.5 us -> 76.8 us (0.82)
  Pallas kernels: 89.2 us -> 75.2 us
  local copies, waits for them, and re-layouts: 4.13 us -> 1.53 us
    pallas_call x1, Pallas kernels: 89.2 us -> 75.2 us  [body(): pl.pallas_call(functools.partial(kernel, (n_p, n_z, rows, sh, cuts, rows...]
    unnamed x5 -> x1, local copies, waits for them, and re-layouts: 4.13 us -> 1.53 us
where the time goes in v2:
time: 76.8 us; the launch traced here: 76.7 us
  Pallas kernels  75.2 us (98%)
  local copies, waits for them, and re-layouts  1.53 us (2%)
    pallas_call x1, Pallas kernels, body(): pl.pallas_call(functools.partial(kernel, (n_p, n_z, rows, sh, cuts, rows...  75.2 us

profile of v2, /device:TPU:1, one launch (start us, length us, event | category | flops | bytes accessed | tf_op | source)
XLA Modules:
  0.0 76.7 jit_solution(8802122965845235710)
XLA Ops:
  0.0 75.2 %cg_solve.1 = f32[152,128]{1,0:T(8,128)} custom-call(f32[1216,8,128]{2,1,0:T(8,128)} %bitcast.5, f32[1216,128]{1,0:T(8,128)} %bitcast.6), custom_call_target="tpu_custom_call" | custom-call | tf_op jit(solution)/shard_map/cg_solve/pallas_call | solution.py:284
  75.2 1.5 %copy.4 = f32[19456]{0:T(1024)} copy(f32[19456]{0:T(1024)} %bitcast.7) | data formatting | bytes 155648

commit v3 on v2

--- a/solution.py
+++ b/solution.py
@@ -9,6 +9,7 @@
 
 DAMPING = 0.001
 PIECES = 4
+AHEAD = 1
 LANES = 128
 MESH = pl.DeviceIdType.MESH
 
@@ -34,22 +35,25 @@
         pl.semaphore_signal(barrier, inc=1, device_id={"walker": lax.rem(me_z + i, n_z)}, device_id_type=MESH)
         return c
 
-    lax.fori_loop(1, n_p, greet_p, 0)
-    lax.fori_loop(1, n_z, greet_z, 0)
-
-    gcopy = pltpu.make_async_copy(g_hbm, gv, load_sem.at[n_z, 0])
-    gcopy.start()
-    loads = []
+    pltpu.make_async_copy(g_hbm, gv, load_sem.at[n_z]).start()
     for k in range(n_z):
+        if k == 1:
+            lax.fori_loop(1, n_p, greet_p, 0)
+            lax.fori_loop(1, n_z, greet_z, 0)
+        at = pl.ds(k * sh, sh)
         for r in range(rows):
-            c = pltpu.make_async_copy(d_hbm.at[pl.ds(k * sh, sh), r, :], dv.at[r, pl.ds(k * sh, sh), :], load_sem.at[k, r])
-            c.start()
-            loads.append(c)
-
-    def accum(vec, others):
+            pltpu.make_async_copy(d_hbm.at[at, r, :], dv.at[r, at, :], load_sem.at[k]).start()
+
+    def loaded(k):
+        part = dv.at[:, pl.ds(pl.multiple_of(k * sh, 8), sh), :]
+        pltpu.make_async_copy(part, part, load_sem.at[k]).wait()
+
+    def accum(vec, others, ready=None):
         n = rows + 1 + len(others)
 
         def shard(k, a):
+            if ready is not None:
+                ready(k)
             out = list(a)
             for i in range(groups):
                 o = pl.multiple_of(k * sh + i * 8, 8)
@@ -75,6 +79,8 @@
         row = jnp.sum(jnp.where(diag, part, 0.0), axis=0, keepdims=True)
         msg[it] = row
         gath[it, me_p] = row
+        if it == 0:
+            pl.semaphore_wait(barrier, n_p - 1 + n_z - 1)
 
         def send(i, c):
             peer = lax.rem(me_p + i, n_p)
@@ -134,7 +140,7 @@
         lo, n = pieces[c]
         return pl.ds(pl.multiple_of(base(k) + lo, 8), n)
 
-    def reduce_scatter(it, t, w, finish):
+    def reduce_scatter(it, t, w, meanwhile, finish):
         wv = [jnp.broadcast_to(w[r:r + 1, :], (8, LANES)) for r in range(rows)]
 
         def copy(way, kind, c, k, hops):
@@ -154,9 +160,14 @@
             for way in range(2):
                 copy(way, 1, c, 3, 1).start()
         project(6, 5, t, wv)
-        for c in range(n_c):
+        meanwhile()
+
+        def direct(c):
             for way in range(2):
                 copy(way, 2, c, 1, 1).start()
+
+        for c in range(AHEAD):
+            direct(c)
         for c in range(n_c):
             for way in range(2):
                 copy(way, 1, c, 3, 1).wait_recv()
@@ -166,6 +177,9 @@
                     s = s + landed(way, 0, c)
                 t[span(signs[way] * 2, c), :] += s
                 copy(way, 3, c, 2, 2).start()
+            if c + AHEAD < n_c:
+                direct(c + AHEAD)
+        scale = finish(None)
         for c in range(n_c):
             s = t[span(0, c), :]
             for way in range(2):
@@ -173,7 +187,7 @@
                 copy(way, 3, c, 2, 2).wait_recv()
                 s = s + (landed(way, 2, c) + landed(way, 3, c))
             t[span(0, c), :] = s
-            finish(c)
+            finish(c, s, scale)
 
     def gather_copy(it, rf, way, kind, c, k, hops):
         piece = rf.at[span(-signs[way] * k, c), :]
@@ -182,16 +196,22 @@
     def gather_start(it, rf, c):
         for way in range(2):
             gather_copy(it, rf, way, 0, c, 0, 2).start()
+
+    def gather_near(it, rf, c):
         for way in range(2):
             gather_copy(it, rf, way, 1, c, 0, 1).start()
 
     def gather_finish(it, rf):
+        for c in range(n_c // 2):
+            gather_near(it, rf, c)
         for c in range(n_c):
             for way in range(2):
                 gather_copy(it, rf, way, 0, c, 0, 2).wait_recv()
                 if c in far[way]:
                     gather_copy(it, rf, way, 3, c, 2, 2).start()
                 gather_copy(it, rf, way, 2, c, 2, 1).start()
+            if c >= n_c // 2:
+                gather_near(it, rf, c)
         for c in range(n_c):
             for way in range(2):
                 gather_copy(it, rf, way, 1, c, 0, 1).wait_recv()
@@ -203,26 +223,22 @@
     inv = 1.0 / rows_all
 
     acc[...] = jnp.zeros_like(acc)
-    gcopy.wait()
-    for c in loads:
-        c.wait()
-    accum(gv, ())
-    pl.semaphore_wait(barrier, n_p - 1 + n_z - 1)
-
+    pltpu.make_async_copy(g_hbm, gv, load_sem.at[n_z]).wait()
+    accum(gv, (), loaded)
     tot = plane_sum(0)
     w0, rr0 = tot[:rows], tot[rows:rows + 1]
     pp0 = rr0
-    z_start(0, w0)
     a0 = []
 
-    def residual1(c):
-        if c == 0:
+    def residual1(c, s=None, a=None):
+        if c is None:
             a0.append(rr0 / (z_finish(0) * inv + DAMPING * pp0))
+            return a0[0]
         at = span(0, c)
-        r1f[at, :] = gv[at, :] - a0[0] * (t1[at, :] * inv + DAMPING * gv[at, :])
+        r1f[at, :] = gv[at, :] - a * (s * inv + DAMPING * gv[at, :])
         gather_start(0, r1f, c)
 
-    reduce_scatter(0, t1, w0, residual1)
+    reduce_scatter(0, t1, w0, lambda: z_start(0, w0), residual1)
     gather_finish(0, r1f)
     accum(r1f, (gv,))
 
@@ -232,18 +248,18 @@
     u1 = tot[:rows]
     w1 = u1 + b0 * w0
     pp1 = rr1 + b0 * (2.0 * rp1 + b0 * pp0)
-    z_start(1, w1)
     a1 = []
 
-    def residual2(c):
-        if c == 0:
+    def residual2(c, s=None, a=None):
+        if c is None:
             a1.append(rr1 / (z_finish(1) * inv + DAMPING * pp1))
+            return a1[0]
         at = span(0, c)
         p1 = r1f[at, :] + b0 * gv[at, :]
-        r2f[at, :] = r1f[at, :] - a1[0] * ((t2[at, :] + b0 * t1[at, :]) * inv + DAMPING * p1)
+        r2f[at, :] = r1f[at, :] - a * ((s + b0 * t1[at, :]) * inv + DAMPING * p1)
         gather_start(1, r2f, c)
 
-    reduce_scatter(1, t2, u1, residual2)
+    reduce_scatter(1, t2, u1, lambda: z_start(1, w1), residual2)
     gather_finish(1, r2f)
     accum(r2f, (gv, r1f))
 
@@ -295,7 +311,7 @@
             pltpu.VMEM((3, n_p, 1, LANES), f32),
             pltpu.VMEM((3, 1, LANES), f32),
             pltpu.VMEM((3, n_z, 1, LANES), f32),
-            pltpu.SemaphoreType.DMA((n_z + 1, rows)),
+            pltpu.SemaphoreType.DMA((n_z + 1,)),
             pltpu.SemaphoreType.DMA((2, 2)),
             pltpu.SemaphoreType.DMA((2, 2, 2, 4, PIECES)),
             pltpu.SemaphoreType.DMA((3,)),

time: 76.8 us -> 74.3 us (0.967)
  Pallas kernels: 75.2 us -> 72.6 us
    pallas_call x1, Pallas kernels: 75.2 us -> 72.6 us  [body(): pl.pallas_call(functools.partial(kernel, (n_p, n_z, rows, sh, cuts, rows...]
where the time goes in v3:
time: 74.3 us; the launch traced here: 74.2 us
  Pallas kernels  72.6 us (98%)
  local copies, waits for them, and re-layouts  1.53 us (2%)
    pallas_call x1, Pallas kernels, body(): pl.pallas_call(functools.partial(kernel, (n_p, n_z, rows, sh, cuts, rows...  72.6 us
    unnamed x1, local copies, waits for them, and re-layouts  1.53 us

profile of v3, /device:TPU:1, one launch (start us, length us, event | category | flops | bytes accessed | tf_op | source)
XLA Modules:
  0.0 74.2 jit_solution(18303060935148208339)
XLA Ops:
  0.0 72.6 %cg_solve.1 = f32[152,128]{1,0:T(8,128)} custom-call(f32[1216,8,128]{2,1,0:T(8,128)} %bitcast.5, f32[1216,128]{1,0:T(8,128)} %bitcast.6), custom_call_target="tpu_custom_call" | custom-call | tf_op jit(solution)/shard_map/cg_solve/pallas_call | solution.py:300
  72.6 1.5 %copy.4 = f32[19456]{0:T(1024)} copy(f32[19456]{0:T(1024)} %bitcast.7) | data formatting | bytes 155648

commit v4 on v3

--- a/solution.py
+++ b/solution.py
@@ -1,4 +1,5 @@
 import functools
+import itertools
 
 import jax
 import jax.numpy as jnp
@@ -9,7 +10,18 @@
 
 DAMPING = 0.001
 PIECES = 4
-AHEAD = 1
+ROUTES = (
+    (0, 0, 0, 4, 3), (0, 0, 1, 3, 2), (0, 0, 0, 2, 1), (0, 1, 1, 4, 3), (0, 1, 0, 3, 2), (0, 1, 1, 2, 1),
+    (0, 2, 0, 4, 3), (0, 2, 1, 3, 2), (0, 2, 0, 2, 1), (0, 3, 1, 4, 3), (0, 3, 0, 3, 2), (0, 3, 1, 2, 1),
+    (0, 0, 1, 1, 0), (0, 1, 0, 1, 0), (0, 2, 1, 1, 0), (0, 3, 0, 1, 0), (0, 0, 0, 3, 0), (0, 0, 1, 2, 0),
+    (0, 0, 0, 1, 0), (0, 1, 1, 3, 0), (0, 1, 0, 2, 0), (0, 1, 1, 1, 0), (0, 2, 0, 3, 0), (0, 2, 1, 2, 0),
+    (0, 3, 1, 3, 0), (0, 2, 0, 1, 0), (0, 3, 1, 1, 0), (0, 3, 0, 2, 0), (1, 0, 0, 0, 2), (1, 0, 0, 0, 1),
+    (1, 0, 1, 0, 2), (1, 0, 1, 0, 1), (1, 1, 0, 0, 2), (1, 1, 1, 0, 2), (1, 2, 0, 0, 2), (1, 2, 1, 0, 2),
+    (1, 3, 0, 0, 2), (1, 3, 1, 0, 2), (1, 0, 0, 2, 4), (1, 0, 0, 2, 3), (1, 0, 1, 2, 3), (1, 1, 0, 0, 1),
+    (1, 1, 1, 0, 1), (1, 1, 0, 2, 3), (1, 1, 1, 2, 4), (1, 1, 1, 2, 3), (1, 2, 0, 0, 1), (1, 2, 1, 0, 1),
+    (1, 2, 0, 2, 4), (1, 2, 0, 2, 3), (1, 2, 1, 2, 3), (1, 3, 0, 0, 1), (1, 3, 1, 0, 1), (1, 3, 0, 2, 3),
+    (1, 3, 1, 2, 4), (1, 3, 1, 2, 3),
+)
 LANES = 128
 MESH = pl.DeviceIdType.MESH
 
@@ -25,11 +37,14 @@
     def base(k):
         return pl.multiple_of(lax.rem(me_z + (k + n_z), n_z) * sh, 8)
 
+    y, x, core = me_p // 8, lax.rem(me_p // 2, 4), lax.rem(me_p, 2)
+    ys, xs, cores = ([lax.rem(at + i, n) for i in range(n)] for at, n in ((y, 4), (x, 4), (core, 2)))
+    plane = [(ys[j] * 4 + xs[i]) * 2 + cores[k]
+             for j, i, k in sorted(itertools.product(range(4), range(4), range(2)),
+                                   key=lambda s: -min(s[0], 4 - s[0]) - min(s[1], 4 - s[1]) - 0.1 * s[2])
+             if (j, i, k) != (0, 0, 0)]
+
     barrier = pltpu.get_barrier_semaphore()
-
-    def greet_p(i, c):
-        pl.semaphore_signal(barrier, inc=1, device_id={"param": lax.rem(me_p + i, n_p)}, device_id_type=MESH)
-        return c
 
     def greet_z(i, c):
         pl.semaphore_signal(barrier, inc=1, device_id={"walker": lax.rem(me_z + i, n_z)}, device_id_type=MESH)
@@ -38,7 +53,8 @@
     pltpu.make_async_copy(g_hbm, gv, load_sem.at[n_z]).start()
     for k in range(n_z):
         if k == 1:
-            lax.fori_loop(1, n_p, greet_p, 0)
+            for peer in plane:
+                pl.semaphore_signal(barrier, inc=1, device_id={"param": peer}, device_id_type=MESH)
             lax.fori_loop(1, n_z, greet_z, 0)
         at = pl.ds(k * sh, sh)
         for r in range(rows):
@@ -48,15 +64,16 @@
         part = dv.at[:, pl.ds(pl.multiple_of(k * sh, 8), sh), :]
         pltpu.make_async_copy(part, part, load_sem.at[k]).wait()
 
-    def accum(vec, others, ready=None):
+    def accum(vec, others, ready=None, first=0, count=None, more=False):
         n = rows + 1 + len(others)
 
         def shard(k, a):
             if ready is not None:
                 ready(k)
+            b = k * sh if first is None else pl.multiple_of(lax.rem(me_z + (first + k), n_z) * sh, 8)
             out = list(a)
             for i in range(groups):
-                o = pl.multiple_of(k * sh + i * 8, 8)
+                o = pl.multiple_of(b + i * 8, 8)
                 v = vec[pl.ds(o, 8), :]
                 for r in range(rows):
                     out[r] = out[r] + dv[r, pl.ds(o, 8), :] * v
@@ -65,7 +82,8 @@
                     out[rows + 1 + j] = out[rows + 1 + j] + ref[pl.ds(o, 8), :] * v
             return tuple(out)
 
-        a = lax.fori_loop(0, n_z, shard, tuple(jnp.zeros((8, LANES), jnp.float32) for _ in range(n)))
+        init = tuple(acc[i] if more else jnp.zeros((8, LANES), jnp.float32) for i in range(n))
+        a = lax.fori_loop(0, n_z if count is None else count, shard, init)
         for i in range(n):
             acc[i] = a[i]
 
@@ -82,13 +100,9 @@
         if it == 0:
             pl.semaphore_wait(barrier, n_p - 1 + n_z - 1)
 
-        def send(i, c):
-            peer = lax.rem(me_p + i, n_p)
+        for peer in plane:
             pltpu.make_async_remote_copy(msg.at[it], gath.at[it, me_p], pl_send.at[it], pl_recv.at[it],
                                          device_id={"param": peer}, device_id_type=MESH).start()
-            return c
-
-        lax.fori_loop(1, n_p, send, 0)
         every = gath.at[it, pl.ds(0, n_p - 1)]
         pltpu.make_async_copy(every, every, pl_recv.at[it]).wait()
         tot = jnp.sum(gath[it, :, 0, :], axis=0, keepdims=True)
@@ -127,120 +141,96 @@
         lax.fori_loop(0, count, shard, 0)
 
     pieces = tuple((cuts[c], cuts[c + 1] - cuts[c]) for c in range(len(cuts) - 1))
-    n_c = len(pieces)
-    far = (range(n_c // 2), range(n_c // 2, n_c))
     signs = (1, -1)
-
-    def ring(it, phase, way, kind, c, hops, src, dst):
-        return pltpu.make_async_remote_copy(
-            src, dst, ring_send.at[it, phase], ring_recv.at[it, phase, way, kind, c],
-            device_id={"walker": lax.rem(me_z + n_z + signs[way] * hops, n_z)}, device_id_type=MESH)
 
     def span(k, c):
         lo, n = pieces[c]
         return pl.ds(pl.multiple_of(base(k) + lo, 8), n)
 
-    def reduce_scatter(it, t, w, meanwhile, finish):
+    def exchange(it, t, w, rf, others, meanwhile, finish):
         wv = [jnp.broadcast_to(w[r:r + 1, :], (8, LANES)) for r in range(rows)]
 
-        def copy(way, kind, c, k, hops):
+        def copy(phase, c, way, a, b):
             lo, n = pieces[c]
-            return ring(it, 0, way, kind, c, hops, t.at[span(signs[way] * k, c), :],
-                        rb.at[it, way, kind, pl.ds(lo, n), :])
-
-        def landed(way, kind, c):
-            lo, n = pieces[c]
-            return rb[it, way, kind, pl.ds(lo, n), :]
-
+            sign = signs[way]
+            if phase == 0:
+                src, dst = t.at[span(sign * a, c), :], rb.at[it, way, a - 1, pl.ds(lo, n), :]
+                slot = a - 1
+            else:
+                src = dst = rf.at[span(-sign * a, c), :]
+                slot = b - 1
+            peer = lax.rem(me_z + (n_z + sign * abs(a - b)), n_z)
+            return pltpu.make_async_remote_copy(
+                src, dst, ring_send.at[it, phase], ring_recv.at[it, phase, way, slot, c],
+                device_id={"walker": peer}, device_id_type=MESH)
+
+        def arrive(phase, c, way, at):
+            total = None
+            for route in ROUTES:
+                if route[:3] == (phase, c, way) and route[4] == at and route not in waited:
+                    waited.add(route)
+                    copy(*route).wait_recv()
+                    if phase == 0:
+                        lo, n = pieces[c]
+                        part = rb[it, way, route[3] - 1, pl.ds(lo, n), :]
+                        total = part if total is None else total + part
+            return total
+
+        waited, done = set(), set()
         project(3, 3, t, wv)
-        for c in range(n_c):
-            for way in range(2):
-                if c in far[way]:
-                    copy(way, 0, c, 4, 2).start()
-            for way in range(2):
-                copy(way, 1, c, 3, 1).start()
-        project(6, 5, t, wv)
-        meanwhile()
-
-        def direct(c):
-            for way in range(2):
-                copy(way, 2, c, 1, 1).start()
-
-        for c in range(AHEAD):
-            direct(c)
-        for c in range(n_c):
-            for way in range(2):
-                copy(way, 1, c, 3, 1).wait_recv()
-                s = landed(way, 1, c)
-                if c in far[way]:
-                    copy(way, 0, c, 4, 2).wait_recv()
-                    s = s + landed(way, 0, c)
-                t[span(signs[way] * 2, c), :] += s
-                copy(way, 3, c, 2, 2).start()
-            if c + AHEAD < n_c:
-                direct(c + AHEAD)
-        scale = finish(None)
-        for c in range(n_c):
-            s = t[span(0, c), :]
-            for way in range(2):
-                copy(way, 2, c, 1, 1).wait_recv()
-                copy(way, 3, c, 2, 2).wait_recv()
-                s = s + (landed(way, 2, c) + landed(way, 3, c))
-            t[span(0, c), :] = s
-            finish(c, s, scale)
-
-    def gather_copy(it, rf, way, kind, c, k, hops):
-        piece = rf.at[span(-signs[way] * k, c), :]
-        return ring(it, 1, way, kind, c, hops, piece, piece)
-
-    def gather_start(it, rf, c):
-        for way in range(2):
-            gather_copy(it, rf, way, 0, c, 0, 2).start()
-
-    def gather_near(it, rf, c):
-        for way in range(2):
-            gather_copy(it, rf, way, 1, c, 0, 1).start()
-
-    def gather_finish(it, rf):
-        for c in range(n_c // 2):
-            gather_near(it, rf, c)
-        for c in range(n_c):
-            for way in range(2):
-                gather_copy(it, rf, way, 0, c, 0, 2).wait_recv()
-                if c in far[way]:
-                    gather_copy(it, rf, way, 3, c, 2, 2).start()
-                gather_copy(it, rf, way, 2, c, 2, 1).start()
-            if c >= n_c // 2:
-                gather_near(it, rf, c)
-        for c in range(n_c):
-            for way in range(2):
-                gather_copy(it, rf, way, 1, c, 0, 1).wait_recv()
-                gather_copy(it, rf, way, 2, c, 2, 1).wait_recv()
-                if c in far[way]:
-                    gather_copy(it, rf, way, 3, c, 2, 2).wait_recv()
+        for phase, c, way, a, b in ROUTES:
+            if phase == 0:
+                if a < 3 and "rest" not in done:
+                    project(6, 5, t, wv)
+                    done.add("rest")
+                s = arrive(0, c, way, a)
+                if s is not None:
+                    t[span(signs[way] * a, c), :] += s
+            elif a == 0:
+                if c not in done:
+                    if "scale" not in done:
+                        finish(None, None)
+                        done.add("scale")
+                    s = t[span(0, c), :]
+                    for w_ in range(2):
+                        s = s + arrive(0, c, w_, 0)
+                    t[span(0, c), :] = s
+                    finish(c, s)
+                    done.add(c)
+            else:
+                arrive(1, c, way, a)
+            copy(phase, c, way, a, b).start()
+            if "z" not in done and "rest" in done:
+                meanwhile()
+                done.add("z")
+        for far in (False, True):
+            for route in ROUTES:
+                if route[0] == 1 and (route[4] > 2) == far:
+                    arrive(1, route[1], route[2], route[4])
+            if far:
+                accum(rf, others, None, 3, 3, True)
+            else:
+                accum(rf, others, None, 6, 5)
 
     own = pl.ds(base(0), sh)
     inv = 1.0 / rows_all
 
     acc[...] = jnp.zeros_like(acc)
     pltpu.make_async_copy(g_hbm, gv, load_sem.at[n_z]).wait()
-    accum(gv, (), loaded)
+    accum(gv, (), loaded, None)
     tot = plane_sum(0)
     w0, rr0 = tot[:rows], tot[rows:rows + 1]
     pp0 = rr0
     a0 = []
 
-    def residual1(c, s=None, a=None):
+    def residual1(c, s):
         if c is None:
             a0.append(rr0 / (z_finish(0) * inv + DAMPING * pp0))
-            return a0[0]
+            return
         at = span(0, c)
-        r1f[at, :] = gv[at, :] - a * (s * inv + DAMPING * gv[at, :])
-        gather_start(0, r1f, c)
-
-    reduce_scatter(0, t1, w0, lambda: z_start(0, w0), residual1)
-    gather_finish(0, r1f)
-    accum(r1f, (gv,))
+        r1f[at, :] = gv[at, :] - a0[0] * (s * inv + DAMPING * gv[at, :])
+
+    exchange(0, t1, w0, r1f, (gv,), lambda: z_start(0, w0), residual1)
 
     tot = plane_sum(1)
     rr1, rp1 = tot[rows:rows + 1], tot[rows + 1:rows + 2]
@@ -250,18 +240,15 @@
     pp1 = rr1 + b0 * (2.0 * rp1 + b0 * pp0)
     a1 = []
 
-    def residual2(c, s=None, a=None):
+    def residual2(c, s):
         if c is None:
             a1.append(rr1 / (z_finish(1) * inv + DAMPING * pp1))
-            return a1[0]
+            return
         at = span(0, c)
         p1 = r1f[at, :] + b0 * gv[at, :]
-        r2f[at, :] = r1f[at, :] - a * ((s + b0 * t1[at, :]) * inv + DAMPING * p1)
-        gather_start(1, r2f, c)
-
-    reduce_scatter(1, t2, u1, lambda: z_start(1, w1), residual2)
-    gather_finish(1, r2f)
-    accum(r2f, (gv, r1f))
+        r2f[at, :] = r1f[at, :] - a1[0] * ((s + b0 * t1[at, :]) * inv + DAMPING * p1)
+
+    exchange(1, t2, u1, r2f, (gv, r1f), lambda: z_start(1, w1), residual2)
 
     tot = plane_sum(2)
     rr2, rg2, rq2 = tot[rows:rows + 1], tot[rows + 1:rows + 2], tot[rows + 2:rows + 3]

time: 74.3 us -> 72.6 us (0.977)
  Pallas kernels: 72.6 us -> 70.9 us
    pallas_call x1, Pallas kernels: 72.6 us -> 70.9 us  [body(): pl.pallas_call(functools.partial(kernel, (n_p, n_z, rows, sh, cuts, rows...]
where the time goes in v4:
time: 72.6 us; the launch traced here: 72.4 us
  Pallas kernels  70.9 us (98%)
  local copies, waits for them, and re-layouts  1.53 us (2%)
    pallas_call x1, Pallas kernels, body(): pl.pallas_call(functools.partial(kernel, (n_p, n_z, rows, sh, cuts, rows...  70.9 us
    unnamed x1, local copies, waits for them, and re-layouts  1.53 us

profile of v4, /device:TPU:1, one launch (start us, length us, event | category | flops | bytes accessed | tf_op | source)
XLA Modules:
  0.0 72.4 jit_solution(12358176865047048847)
XLA Ops:
  0.0 70.9 %cg_solve.1 = f32[152,128]{1,0:T(8,128)} custom-call(f32[1216,8,128]{2,1,0:T(8,128)} %bitcast.5, f32[1216,128]{1,0:T(8,128)} %bitcast.6), custom_call_target="tpu_custom_call" | custom-call | tf_op jit(solution)/shard_map/cg_solve/pallas_call | solution.py:287
  70.9 1.5 %copy.4 = f32[19456]{0:T(1024)} copy(f32[19456]{0:T(1024)} %bitcast.7) | data formatting | bytes 155648

commit v5 on v4

--- a/solution.py
+++ b/solution.py
@@ -13,9 +13,9 @@
 ROUTES = (
     (0, 0, 0, 4, 3), (0, 0, 1, 3, 2), (0, 0, 0, 2, 1), (0, 1, 1, 4, 3), (0, 1, 0, 3, 2), (0, 1, 1, 2, 1),
     (0, 2, 0, 4, 3), (0, 2, 1, 3, 2), (0, 2, 0, 2, 1), (0, 3, 1, 4, 3), (0, 3, 0, 3, 2), (0, 3, 1, 2, 1),
-    (0, 0, 1, 1, 0), (0, 1, 0, 1, 0), (0, 2, 1, 1, 0), (0, 3, 0, 1, 0), (0, 0, 0, 3, 0), (0, 0, 1, 2, 0),
-    (0, 0, 0, 1, 0), (0, 1, 1, 3, 0), (0, 1, 0, 2, 0), (0, 1, 1, 1, 0), (0, 2, 0, 3, 0), (0, 2, 1, 2, 0),
-    (0, 3, 1, 3, 0), (0, 2, 0, 1, 0), (0, 3, 1, 1, 0), (0, 3, 0, 2, 0), (1, 0, 0, 0, 2), (1, 0, 0, 0, 1),
+    (0, 0, 1, 1, 0), (0, 1, 0, 1, 0), (0, 0, 0, 3, 0), (0, 0, 1, 2, 0), (0, 0, 0, 1, 0), (0, 1, 1, 3, 0),
+    (0, 1, 0, 2, 0), (0, 1, 1, 1, 0), (0, 2, 0, 3, 0), (0, 2, 1, 2, 0), (0, 2, 1, 1, 0), (0, 3, 1, 3, 0),
+    (0, 2, 0, 1, 0), (0, 3, 1, 1, 0), (0, 3, 0, 2, 0), (0, 3, 0, 1, 0), (1, 0, 0, 0, 2), (1, 0, 0, 0, 1),
     (1, 0, 1, 0, 2), (1, 0, 1, 0, 1), (1, 1, 0, 0, 2), (1, 1, 1, 0, 2), (1, 2, 0, 0, 2), (1, 2, 1, 0, 2),
     (1, 3, 0, 0, 2), (1, 3, 1, 0, 2), (1, 0, 0, 2, 4), (1, 0, 0, 2, 3), (1, 0, 1, 2, 3), (1, 1, 0, 0, 1),
     (1, 1, 1, 0, 1), (1, 1, 0, 2, 3), (1, 1, 1, 2, 4), (1, 1, 1, 2, 3), (1, 2, 0, 0, 1), (1, 2, 1, 0, 1),

time: 72.6 us -> 72.3 us (level)
  no operation moved by 1% of the time
where the time goes in v5:
time: 72.3 us; the launch traced here: 72.2 us
  Pallas kernels  70.6 us (98%)
  local copies, waits for them, and re-layouts  1.53 us (2%)
    pallas_call x1, Pallas kernels, body(): pl.pallas_call(functools.partial(kernel, (n_p, n_z, rows, sh, cuts, rows...  70.6 us
    unnamed x1, local copies, waits for them, and re-layouts  1.53 us

profile of v5, /device:TPU:1, one launch (start us, length us, event | category | flops | bytes accessed | tf_op | source)
XLA Modules:
  0.0 72.2 jit_solution(12202062345590123843)
XLA Ops:
  0.0 70.6 %cg_solve.1 = f32[152,128]{1,0:T(8,128)} custom-call(f32[1216,8,128]{2,1,0:T(8,128)} %bitcast.5, f32[1216,128]{1,0:T(8,128)} %bitcast.6), custom_call_target="tpu_custom_call" | custom-call | tf_op jit(solution)/shard_map/cg_solve/pallas_call | solution.py:287
  70.6 1.5 %copy.4 = f32[19456]{0:T(1024)} copy(f32[19456]{0:T(1024)} %bitcast.7) | data formatting | bytes 155648

commit v6 on v5

--- a/solution.py
+++ b/solution.py
@@ -12,15 +12,15 @@
 PIECES = 4
 ROUTES = (
     (0, 0, 0, 4, 3), (0, 0, 1, 3, 2), (0, 0, 0, 2, 1), (0, 1, 1, 4, 3), (0, 1, 0, 3, 2), (0, 1, 1, 2, 1),
-    (0, 2, 0, 4, 3), (0, 2, 1, 3, 2), (0, 2, 0, 2, 1), (0, 3, 1, 4, 3), (0, 3, 0, 3, 2), (0, 3, 1, 2, 1),
-    (0, 0, 1, 1, 0), (0, 1, 0, 1, 0), (0, 0, 0, 3, 0), (0, 0, 1, 2, 0), (0, 0, 0, 1, 0), (0, 1, 1, 3, 0),
-    (0, 1, 0, 2, 0), (0, 1, 1, 1, 0), (0, 2, 0, 3, 0), (0, 2, 1, 2, 0), (0, 2, 1, 1, 0), (0, 3, 1, 3, 0),
-    (0, 2, 0, 1, 0), (0, 3, 1, 1, 0), (0, 3, 0, 2, 0), (0, 3, 0, 1, 0), (1, 0, 0, 0, 2), (1, 0, 0, 0, 1),
+    (0, 2, 1, 4, 3), (0, 2, 0, 3, 2), (0, 2, 1, 2, 1), (0, 3, 0, 4, 3), (0, 3, 1, 3, 2), (0, 3, 0, 2, 1),
+    (0, 0, 1, 1, 0), (0, 1, 0, 1, 0), (0, 3, 1, 1, 0), (0, 0, 0, 3, 0), (0, 0, 1, 2, 0), (0, 0, 0, 1, 0),
+    (0, 1, 1, 3, 0), (0, 1, 0, 2, 0), (0, 2, 0, 1, 0), (0, 1, 1, 1, 0), (0, 2, 0, 2, 0), (0, 2, 1, 3, 0),
+    (0, 3, 0, 3, 0), (0, 2, 1, 1, 0), (0, 3, 0, 1, 0), (0, 3, 1, 2, 0), (1, 0, 0, 0, 2), (1, 0, 0, 0, 1),
     (1, 0, 1, 0, 2), (1, 0, 1, 0, 1), (1, 1, 0, 0, 2), (1, 1, 1, 0, 2), (1, 2, 0, 0, 2), (1, 2, 1, 0, 2),
     (1, 3, 0, 0, 2), (1, 3, 1, 0, 2), (1, 0, 0, 2, 4), (1, 0, 0, 2, 3), (1, 0, 1, 2, 3), (1, 1, 0, 0, 1),
     (1, 1, 1, 0, 1), (1, 1, 0, 2, 3), (1, 1, 1, 2, 4), (1, 1, 1, 2, 3), (1, 2, 0, 0, 1), (1, 2, 1, 0, 1),
-    (1, 2, 0, 2, 4), (1, 2, 0, 2, 3), (1, 2, 1, 2, 3), (1, 3, 0, 0, 1), (1, 3, 1, 0, 1), (1, 3, 0, 2, 3),
-    (1, 3, 1, 2, 4), (1, 3, 1, 2, 3),
+    (1, 2, 0, 2, 3), (1, 2, 1, 2, 4), (1, 2, 1, 2, 3), (1, 3, 0, 0, 1), (1, 3, 1, 0, 1), (1, 3, 0, 2, 4),
+    (1, 3, 0, 2, 3), (1, 3, 1, 2, 3),
 )
 LANES = 128
 MESH = pl.DeviceIdType.MESH

time: 72.3 us -> 72.5 us (level)
  no operation moved by 1% of the time
where the time goes in v6:
time: 72.5 us; the launch traced here: 72.4 us
  Pallas kernels  70.9 us (98%)
  local copies, waits for them, and re-layouts  1.53 us (2%)
    pallas_call x1, Pallas kernels, body(): pl.pallas_call(functools.partial(kernel, (n_p, n_z, rows, sh, cuts, rows...  70.9 us
    unnamed x1, local copies, waits for them, and re-layouts  1.53 us

profile of v6, /device:TPU:1, one launch (start us, length us, event | category | flops | bytes accessed | tf_op | source)
XLA Modules:
  0.0 72.4 jit_solution(12717954136405018489)
XLA Ops:
  0.0 70.9 %cg_solve.1 = f32[152,128]{1,0:T(8,128)} custom-call(f32[1216,8,128]{2,1,0:T(8,128)} %bitcast.5, f32[1216,128]{1,0:T(8,128)} %bitcast.6), custom_call_target="tpu_custom_call" | custom-call | tf_op jit(solution)/shard_map/cg_solve/pallas_call | solution.py:287
  70.9 1.5 %copy.4 = f32[19456]{0:T(1024)} copy(f32[19456]{0:T(1024)} %bitcast.7) | data formatting | bytes 155648
